TPU v7x, 128 devices: a whole 4x4x4 slice. The times are simulated.
128 devices in a mesh: ctx: 8 (over x, z_hi), frame: 16 (over z_lo, y, core).
Axes of the slice: x: 4, y: 4, z: 4 (z_hi: 2, z_lo: 2; z = z_hi * 2 + z_lo), core: 2. Of those that a mesh axis runs over, the one named last changes fastest.
Arguments:
- queries: bfloat16 [4096, 4096], P('ctx', 'frame'), may hold values from -160 to 160
- keys: bfloat16 [8192, 4096], P('ctx', 'frame'), may hold values from -4 to 4
- values: bfloat16 [8192, 4096], P('ctx', 'frame'), may hold values from -6 to 6
- query_frames: int32 [256], P('ctx'), may hold values from 0 to 383, as said below
- frame_counts: int32 [512], replicated, may hold values from 0 to 16, as said below
- clip_of_frame: int32 [256], P('ctx'), may hold values from 0 to 15, as said below
- in_proj: bfloat16 [4096, 1024], P('frame'), may hold values from -0.09375 to 0.09375
- mlp_up: bfloat16 [1024, 4096], replicated, may hold values from -0.1875 to 0.1875
- mlp_down: bfloat16 [4096, 1024], replicated, may hold values from -0.09375 to 0.09375
- reward_head: float32 [1024], replicated, may hold values from -0.1875 to 0.1875
Outputs:
- query_grad: float32 [4096, 4096], P('ctx', 'frame')
- key_grad: float32 [8192, 4096], P('ctx', 'frame')
- value_grad: float32 [8192, 4096], P('ctx', 'frame')
- clip_reward: float32 [128], P(('ctx', 'frame'))
Inputs may be any that keep to these rules, and one draw needn't show every extreme that they name: `query_frames`: the query patch rows are distinct rows of the first 512 * 3 // 4 patch rows of the video, in increasing order, all of them live; the first and the last of those rows are always among them. `frame_counts`: the live tokens are a prefix of the sequence of at least three quarters of it: rows before the prefix's end are full, one row may be partly live, the rows after it have none, and the last row has none. `clip_of_frame`: within each aligned block of 32 patch row slots every clip number appears exactly 2 times.
All inputs are finite; a program needn't handle non-finite values.
Results may differ from a plain program's by a relative error of at most 0.02.
Values may be sent and summed in bfloat16 or wider, within the bound.
No kernel may reach another device: no remote copies, remote signals or barrier semaphores. Data moves between devices by JAX's collectives and lax.ppermute only.
A program may use at most 192 MiB of HBM per device.

v0:
```python
import functools
import math
import jax
import jax.numpy as jnp
from jax import lax
from jax.sharding import PartitionSpec as P

HD = 128
FTOK = 16
CLIP = 2
EPSILON = 1e-05


def rotate(values_in, position, inverse):
    row_count = values_in.shape[0]
    half_width = HD // 2
    pieces = values_in.reshape(row_count, -1, HD)
    frequency = jnp.exp(-math.log(10000.0) * jnp.arange(half_width, dtype=jnp.float32) / half_width)
    angle = position.astype(jnp.float32)[:, None] * frequency[None, :]
    cosine = jnp.cos(angle)[:, None, :]
    sine = jnp.sin(angle)[:, None, :]
    if inverse:
        sine = -sine
    first_half = pieces[:, :, :half_width]
    second_half = pieces[:, :, half_width:]
    result = jnp.concatenate(
        [first_half * cosine - second_half * sine, second_half * cosine + first_half * sine], axis=2
    )
    return result.reshape(row_count, -1)


def normalize(values_in):
    center = jnp.mean(values_in, axis=-1, keepdims=True)
    centered = values_in - center
    variance = jnp.mean(centered * centered, axis=-1, keepdims=True)
    return centered * lax.rsqrt(variance + EPSILON)


def head_scores(query_head, key_head, key_valid):
    scores = jnp.dot(query_head, key_head.T, preferred_element_type=jnp.float32) * (
        1.0 / math.sqrt(HD)
    )
    return jnp.where(key_valid[None, :], scores, -jnp.inf)


def contract_rows(left, right):
    return lax.dot_general(
        left, right, (((0,), (0,)), ((), ())), preferred_element_type=jnp.float32
    )


def score_clip(inputs, clip_live, mlp_up, mlp_down, reward_head):
    normed = normalize(inputs).astype(jnp.bfloat16)
    expanded = jax.nn.gelu(jnp.dot(normed, mlp_up, preferred_element_type=jnp.float32)).astype(
        jnp.bfloat16
    )
    hidden = jnp.dot(expanded, mlp_down, preferred_element_type=jnp.float32)
    live = clip_live.astype(jnp.float32)
    count = jnp.sum(live)
    pooled = jnp.sum(hidden * live[:, None], axis=0) / count
    return count * jnp.dot(normalize(pooled), reward_head, precision=lax.Precision.HIGHEST)


def shards(
    queries,
    keys,
    values,
    query_frames,
    frame_counts,
    clip_of_frame,
    in_proj,
    mlp_up,
    mlp_down,
    reward_head,
):
    ctx_index = lax.axis_index("ctx")
    frame_index = lax.axis_index("frame")
    query_rows = queries.shape[0]
    key_rows = keys.shape[0]
    frame_slots = query_frames.shape[0]
    width_dev = queries.shape[1]
    head_count = width_dev // HD
    key_frames = frame_counts.shape[0]
    scale = 1.0 / math.sqrt(HD)
    in_frame = jnp.arange(FTOK, dtype=jnp.int32)
    query_position = (query_frames[:, None] * FTOK + in_frame[None, :]).reshape(-1)
    key_position = ctx_index * key_rows + jnp.arange(key_rows, dtype=jnp.int32)
    key_valid = (in_frame[None, :] < frame_counts[:, None]).reshape(-1)
    frame_match = query_frames[:, None] == jnp.arange(key_frames, dtype=jnp.int32)[None, :]
    slot_counts = jnp.sum(jnp.where(frame_match, frame_counts[None, :], 0), axis=1)
    rotated_query = rotate(queries.astype(jnp.float32), query_position, False).astype(jnp.bfloat16)
    rotated_key = rotate(keys.astype(jnp.float32), key_position, False).astype(jnp.bfloat16)
    whole_key, whole_value = (
        lax.all_gather(rotated_key, "ctx", axis=0, tiled=True),
        lax.all_gather(values, "ctx", axis=0, tiled=True),
    )
    out_list, log_list, weight_list = ([], [], [])
    for head_number in range(head_count):
        lower = head_number * HD
        scores = head_scores(
            rotated_query[:, lower : lower + HD], whole_key[:, lower : lower + HD], key_valid
        )
        largest = jnp.max(scores, axis=1)
        total = jnp.sum(jnp.exp(scores - largest[:, None]), axis=1)
        log_total = largest + jnp.log(total)
        weights = jnp.exp(scores - log_total[:, None])
        out_list.append(
            jnp.dot(
                weights.astype(jnp.bfloat16),
                whole_value[:, lower : lower + HD],
                preferred_element_type=jnp.float32,
            ).astype(jnp.bfloat16)
        )
        log_list.append(log_total)
        weight_list.append(weights)
    attention_out = jnp.concatenate(out_list, axis=1)
    slot_index = jnp.arange(frame_slots, dtype=jnp.int32)
    same_clip = clip_of_frame[:, None] == clip_of_frame[None, :]
    earlier = slot_index[None, :] < slot_index[:, None]
    rank = jnp.sum(jnp.logical_and(same_clip, earlier), axis=1)
    destination = clip_of_frame * CLIP + rank
    source = jnp.sum(
        jnp.where(destination[None, :] == slot_index[:, None], slot_index[None, :], 0), axis=1
    )

    def regroup(array, order):
        framed = array.reshape(frame_slots, FTOK, array.shape[1])
        return jnp.take(framed, order, axis=0).reshape(query_rows, array.shape[1])

    grouped_out = regroup(attention_out, source)
    my_slots = lax.dynamic_slice_in_dim(source, frame_index * CLIP, CLIP)
    my_match = my_slots[:, None] == slot_index[None, :]
    my_counts = jnp.sum(jnp.where(my_match, slot_counts[None, :], 0), axis=1)
    clip_live = (in_frame[None, :] < my_counts[:, None]).reshape(-1)
    clip_inputs = lax.psum_scatter(
        jnp.dot(grouped_out, in_proj, preferred_element_type=jnp.float32),
        "frame",
        scatter_dimension=0,
        tiled=True,
    )
    scorer = functools.partial(
        score_clip, clip_live=clip_live, mlp_up=mlp_up, mlp_down=mlp_down, reward_head=reward_head
    )
    clip_value, pull_back = jax.vjp(scorer, clip_inputs)
    (input_grad,) = pull_back(jnp.ones_like(clip_value))
    low_grad = input_grad.astype(jnp.bfloat16)
    grouped_grad = jnp.dot(
        lax.all_gather(low_grad, "frame", axis=0, tiled=True),
        in_proj.T,
        preferred_element_type=jnp.float32,
    ).astype(jnp.bfloat16)
    out_grad = regroup(grouped_grad, destination)
    delta_list = []
    for head_number in range(head_count):
        lower = head_number * HD
        delta_list.append(
            jnp.sum(
                out_grad[:, lower : lower + HD].astype(jnp.float32)
                * attention_out[:, lower : lower + HD].astype(jnp.float32),
                axis=1,
            )
        )
    query_parts, grad_list, low_list = ([], [], [])
    for head_number in range(head_count):
        lower = head_number * HD
        weights = weight_list[head_number]
        weight_grad = jnp.dot(
            out_grad[:, lower : lower + HD],
            whole_value[:, lower : lower + HD].T,
            preferred_element_type=jnp.float32,
        )
        score_grad = (weights * (weight_grad - delta_list[head_number][:, None]) * scale).astype(
            jnp.bfloat16
        )
        query_parts.append(
            jnp.dot(
                score_grad, whole_key[:, lower : lower + HD], preferred_element_type=jnp.float32
            )
        )
        grad_list.append(score_grad)
        low_list.append(weights.astype(jnp.bfloat16))
    rotated_query_grad = jnp.concatenate(query_parts, axis=1)
    key_parts = []
    value_parts = []
    for head_number in range(head_count):
        lower = head_number * HD
        grad_cols = grad_list[head_number]
        weight_cols = low_list[head_number]
        key_parts.append(contract_rows(grad_cols, rotated_query[:, lower : lower + HD]))
        value_parts.append(contract_rows(weight_cols, out_grad[:, lower : lower + HD]))
    key_both = lax.psum_scatter(
        jnp.concatenate(key_parts + value_parts, axis=1), "ctx", scatter_dimension=0, tiled=True
    )
    rotated_key_grad = key_both[:, :width_dev]
    value_grad = key_both[:, width_dev:]
    query_grad = rotate(rotated_query_grad, query_position, True)
    key_grad = rotate(rotated_key_grad, key_position, True)
    return (query_grad, key_grad, value_grad, clip_value.reshape(1))


def solution(mesh):
    return jax.shard_map(
        shards,
        mesh=mesh,
        in_specs=(
            P("ctx", "frame"),
            P("ctx", "frame"),
            P("ctx", "frame"),
            P("ctx"),
            P(),
            P("ctx"),
            P("frame", None),
            P(),
            P(),
            P(),
        ),
        out_specs=(P("ctx", "frame"), P("ctx", "frame"), P("ctx", "frame"), P(("ctx", "frame"))),
        check_vma=False,
    )
```

profile of v0, /device:TPU:0, one launch (start us, length us, event | category | flops | bytes accessed | tf_op | source)
XLA Modules:
  0.0 561.1 jit_solution(8665673020066702519)
XLA Ops:
  8.6 1.8 fusion.60
  19.1 67.0 %all-gather.4.cloned.1.call-done = bf16[8192,256]{0,1:T(8,128)(2,1)} async-done(((bf16[1024,256]{0,1:T(8,128)(2,1)}), bf16[8192,256]{0,1:T(8,128)(2,1)}) %all-gather.4.cloned.1.call-update) | async-done | bytes 4194320 | tf_op jit(solution)/shard_map/all_gather | solution.py:94
  86.1 8.9 %fusion.94 = (f32[512]{0:T(512)S(1)}, f32[512,8192]{1,0:T(8,128)}) fusion(bf16[8192,256]{0,1:T(8,128)(2,1)} %all-gather.4.cloned.1.call-done, bf16[512,256]{0,1:T(8,128)(2,1)S(1)} %bitcast.41, pred[8192]{0:T(1024)(128)(4,1)S(1)} %lt.69), kind=kOutput, calls=%fused_computation.162 | convolution fusion | flops 1086324224 | bytes 19015680 | tf_op jit(solution)/shard_map/dot_general | solution.py:40
  95.0 8.7 %exponential_reduce_fusion = f32[512]{0:T(512)S(1)} fusion(f32[512,8192]{1,0:T(8,128)} %get-tuple-element.42, f32[512]{0:T(512)S(1)} %get-tuple-element.41), kind=kLoop, calls=%fused_computation.6 | loop fusion | flops 8388096 | bytes 16781312 | tf_op jit(solution)/shard_map/reduce_sum | solution.py:104
  103.7 7.2 %fusion.95 = (f32[512]{0:T(512)S(1)}, f32[512,8192]{1,0:T(8,128)}) fusion(bf16[8192,256]{0,1:T(8,128)(2,1)S(1)} %copy-done.10, bf16[512,256]{0,1:T(8,128)(2,1)S(1)} %bitcast.42, pred[8192]{0:T(1024)(128)(4,1)S(1)} %lt.69), kind=kOutput, calls=%fused_computation.163 | convolution fusion | flops 1086324224 | bytes 19015680 | tf_op jit(solution)/shard_map/dot_general | solution.py:40
  110.9 8.1 %exponential_reduce_fusion.1 = f32[512]{0:T(512)S(1)} fusion(f32[512,8192]{1,0:T(8,128)} %get-tuple-element.44, f32[512]{0:T(512)S(1)} %get-tuple-element.43), kind=kLoop, calls=%fused_computation.9 | loop fusion | flops 8388096 | bytes 16781312 | tf_op jit(solution)/shard_map/reduce_sum | solution.py:104
  119.1 10.2 %fusion.1 = bf16[512,8192]{1,0:T(8,128)(2,1)} fusion(f32[512,8192]{1,0:T(8,128)} %get-tuple-element.42, f32[512]{0:T(512)S(1)} %log_add_fusion), kind=kLoop, calls=%fused_computation.12 | loop fusion | flops 8388608 | bytes 25167872 | tf_op jit(solution)/shard_map/convert_element_type | solution.py:109
  129.3 4.0 copy-done.2
  133.3 5.0 fusion
  138.3 19.5 %all-gather.6.cloned.1.call-done = bf16[8192,256]{1,0:T(8,128)(2,1)} async-done(((bf16[1024,256]{1,0:T(8,128)(2,1)}), bf16[8192,256]{1,0:T(8,128)(2,1)}) %all-gather.6.cloned.1.call-update) | async-done | bytes 4194320 | tf_op jit(solution)/shard_map/all_gather | solution.py:95
  157.8 7.0 %fusion.18 = bf16[512,128]{0,1:T(8,128)(2,1)S(1)} fusion(bf16[512,8192]{1,0:T(8,128)(2,1)} %fusion.1, bf16[8192,256]{1,0:T(8,128)(2,1)} %all-gather.6.cloned.1.call-done), kind=kOutput, calls=%fused_computation.29 | convolution fusion | flops 1073807360 | bytes 10616832 | tf_op jit(solution)/shard_map/dot_general | solution.py:108
  164.8 4.5 fusion.15
  170.3 1.8 fusion.98
  173.4 60.6 %reduce-scatter.3.cloned.1.call-done = f32[32,1024]{1,0:T(8,128)} async-done(((f32[512,1024]{1,0:T(8,128)}), f32[32,1024]{1,0:T(8,128)}) %reduce-scatter.3.cloned.1.call-update) | async-done | bytes 131088 | tf_op jit(solution)/shard_map/reduce_scatter | solution.py:135
  236.1 5.0 fusion.61
  241.2 4.9 fusion.22
  254.5 11.0 %multiply_reduce_fusion.2 = (f32[32]{0:T(128)S(1)}, f32[32,1024]{1,0:T(8,128)S(1)}) fusion(f32[32,1024]{1,0:T(8,128)S(1)} %copy-done.9, f32[32]{0:T(128)S(1)} %broadcast_multiply_fusion, bf16[1024,4096]{1,0:T(8,128)(2,1)} %param.19, f32[32,4096]{1,0:T(8,128)S(1)} %fusion.61, bf16[4096,1024]{1,0:T(8,128)(2,1)} %param.20, f32[1024]{0:T(1024)S(1)} %add_divide_fusion, ...), kind=kOutput, calls=%fused_computation.89 | convolution fusion | flops 539820032 | bytes 17568128 | tf_op jit(solution)/shard_map/transpose(jvp())/dot_general | solution.py:54
  266.7 30.9 %all-gather.8.cloned.1.call-done = bf16[512,1024]{1,0:T(8,128)(2,1)} async-done(((bf16[32,1024]{1,0:T(8,128)(2,1)}), bf16[512,1024]{1,0:T(8,128)(2,1)}) %all-gather.8.cloned.1.call-update) | async-done | bytes 1048592 | tf_op jit(solution)/shard_map/all_gather | solution.py:148
  297.7 1.7 convolution_convert_fusion.1
  300.1 6.6 %fusion.88 = f32[8192,128]{0,1:T(8,128)} fusion(bf16[512,8192]{1,0:T(8,128)(2,1)} %fusion, bf16[512,256]{1,0:T(8,128)(2,1)S(1)} %bitcast.33), kind=kOutput, calls=%fused_computation.156 | convolution fusion | flops 1073741824 | bytes 12713984 | tf_op jit(solution)/shard_map/dot_general | solution.py:47
  306.7 6.6 %fusion.85 = f32[8192,128]{0,1:T(8,128)} fusion(bf16[512,8192]{1,0:T(8,128)(2,1)} %fusion.1, bf16[512,256]{1,0:T(8,128)(2,1)S(1)} %bitcast.34), kind=kOutput, calls=%fused_computation.153 | convolution fusion | flops 1073741824 | bytes 12713984 | tf_op jit(solution)/shard_map/dot_general | solution.py:47
  313.7 8.6 %multiply_convert_fusion = bf16[512,8192]{1,0:T(8,128)(2,1)S(1)} fusion(f32[512,8192]{1,0:T(8,128)} %get-tuple-element.42, f32[512]{0:T(512)S(1)} %multiply_reduce_fusion, f32[512]{0:T(512)S(1)} %log_add_fusion, bf16[8192,256]{1,0:T(8,128)(2,1)} %all-gather.6.cloned.1.call-done, bf16[512,256]{1,0:T(8,128)(2,1)S(1)} %bitcast.36), kind=kOutput, calls=%fused_computation.3 | convolution fusion | flops 1094713344 | bytes 27398144 | tf_op jit(solution)/shard_map/dot_general | solution.py:167
  322.3 3.3 fusion.54
  325.6 1.9 copy-done.5
  327.5 10.4 %multiply_convert_fusion.1 = bf16[512,8192]{1,0:T(8,128)(2,1)} fusion(f32[512,8192]{1,0:T(8,128)} %get-tuple-element.44, f32[512]{0:T(512)S(1)} %multiply_reduce_fusion.1, f32[512]{0:T(512)S(1)} %log_add_fusion.1, bf16[8192,256]{1,0:T(8,128)(2,1)S(1)} %copy-done.5, bf16[512,256]{1,0:T(8,128)(2,1)S(1)} %bitcast.37), kind=kOutput, calls=%fused_computation.4 | convolution fusion | flops 1094713344 | bytes 27398144 | tf_op jit(solution)/shard_map/dot_general | solution.py:167
  338.0 7.0 %fusion.57 = f32[8192,128]{0,1:T(8,128)} fusion(bf16[512,8192]{1,0:T(8,128)(2,1)} %multiply_convert_fusion.1, bf16[512,256]{0,1:T(8,128)(2,1)S(1)} %bitcast.44), kind=kOutput, calls=%fused_computation.96 | convolution fusion | flops 1073741824 | bytes 12713984 | tf_op jit(solution)/shard_map/dot_general | solution.py:47
  345.0 1.5 copy-done.8
  346.5 8.2 %pad_maximum_fusion = f32[8192,512]{0,1:T(8,128)} fusion(f32[8192,128]{0,1:T(8,128)S(1)} %copy-done.7, f32[8192,128]{0,1:T(8,128)S(1)} %copy-done.6, f32[8192,128]{0,1:T(8,128)S(1)} %copy-done.8, f32[8192,128]{0,1:T(8,128)} %fusion.57), kind=kLoop, calls=%fused_computation.2 | loop fusion | flops 12582912 | bytes 33554432 | tf_op jit(solution)/shard_map/concatenate | solution.py:192
  356.0 7.0 %fusion.6 = f32[512,128]{0,1:T(8,128)S(1)} fusion(bf16[512,8192]{1,0:T(8,128)(2,1)} %copy-done.4, bf16[8192,256]{0,1:T(8,128)(2,1)} %all-gather.4.cloned.1.call-done), kind=kOutput, calls=%fused_computation.18 | convolution fusion | flops 1073741824 | bytes 10747904 | tf_op jit(solution)/shard_map/dot_general | solution.py:176
  363.1 7.1 %fusion.12 = f32[512,128]{0,1:T(8,128)S(1)} fusion(bf16[512,8192]{1,0:T(8,128)(2,1)} %multiply_convert_fusion.1, bf16[8192,256]{0,1:T(8,128)(2,1)S(1)} %copy-done.11), kind=kOutput, calls=%fused_computation.24 | convolution fusion | flops 1073741824 | bytes 10747904 | tf_op jit(solution)/shard_map/dot_general | solution.py:176
  371.4 177.3 %reduce-scatter.5.cloned.1.call-done = f32[1024,512]{0,1:T(8,128)} async-done(((f32[8192,512]{0,1:T(8,128)}), f32[1024,512]{0,1:T(8,128)}) %reduce-scatter.5.cloned.1.call-update) | async-done | bytes 2097168 | tf_op jit(solution)/shard_map/reduce_scatter | solution.py:191
  548.6 1.7 fusion.92
  (117 shorter events, 26.5 us)
Async XLA Ops:
  7.2 163.1 %copy-start = (bf16[256,1024]{1,0:T(8,128)(2,1)S(1)}, bf16[256,1024]{1,0:T(8,128)(2,1)}, u32[]{:S(2)}) copy-start(bf16[256,1024]{1,0:T(8,128)(2,1)} %param.18) | copy-start | bytes 1572868
  7.2 78.9 %all-gather.4.cloned.1.call-start = ((), (), s32[]{:S(2)}) async-start(), calls=%async_computation.2 | async-start | bytes 4718592 | tf_op jit(solution)/shard_map/all_gather | solution.py:94
  10.3 0.7 copy-start.12
  11.9 145.9 %all-gather.6.cloned.1.call-start = ((), (), s32[]{:S(2)}) async-start(), calls=%async_computation.3 | async-start | bytes 4718592 | tf_op jit(solution)/shard_map/all_gather | solution.py:95
  12.6 221.4 %reduce-scatter.3.cloned.1.call-start = ((), (), s32[]{:S(2)}) async-start(), calls=%async_computation.4 | async-start | bytes 2228224 | tf_op jit(solution)/shard_map/reduce_scatter | solution.py:135
  14.3 0.6 copy-start.20
  14.4 0.5 copy-start.22
  95.0 8.7 %copy-start.10 = (bf16[8192,256]{0,1:T(8,128)(2,1)S(1)}, bf16[8192,256]{0,1:T(8,128)(2,1)}, u32[]{:S(2)}) copy-start(bf16[8192,256]{0,1:T(8,128)(2,1)} %all-gather.4.cloned.1.call-done) | copy-start | bytes 12582916
  119.1 14.2 %copy-start.2 = (f32[512,8192]{1,0:T(8,128)S(1)}, f32[512,8192]{1,0:T(8,128)}, u32[]{:S(2)}) copy-start(f32[512,8192]{1,0:T(8,128)} %get-tuple-element.44) | copy-start | bytes 50331652
  157.8 7.0 %copy-start.3 = (bf16[512,8192]{1,0:T(8,128)(2,1)S(1)}, bf16[512,8192]{1,0:T(8,128)(2,1)}, u32[]{:S(2)}) copy-start(bf16[512,8192]{1,0:T(8,128)(2,1)} %fusion) | copy-start | bytes 25165828
  164.8 5.3 copy-start.18
  164.8 7.3 %copy-start.23 = (s32[32]{0:T(128)S(1)}, s32[32]{0:T(128)}, u32[]{:S(2)}) copy-start(s32[32]{0:T(128)} %copy-done.22) | copy-start | bytes 388
  164.8 7.4 %copy-start.17 = (s32[512]{0:T(512)S(1)}, s32[512]{0:T(512)}, u32[]{:S(2)}) copy-start(s32[512]{0:T(512)} %param.16) | copy-start | bytes 6148
  164.8 7.4 %copy-start.19 = (s32[32]{0:T(128)S(1)}, s32[32]{0:T(128)}, u32[]{:S(2)}) copy-start(s32[32]{0:T(128)} %param.15) | copy-start | bytes 388
  172.1 125.6 %all-gather.8.cloned.1.call-start = ((), (), s32[]{:S(2)}) async-start(), calls=%async_computation.5 | async-start | bytes 1114112 | tf_op jit(solution)/shard_map/all_gather | solution.py:148
  241.2 8.9 %copy-start.16 = (f32[1024]{0:T(1024)S(1)}, f32[1024]{0:T(1024)}, u32[]{:S(2)}) copy-start(f32[1024]{0:T(1024)} %param.21) | copy-start | bytes 12292
  241.2 13.3 %copy-start.9 = (f32[32,1024]{1,0:T(8,128)S(1)}, f32[32,1024]{1,0:T(8,128)}, u32[]{:S(2)}) copy-start(f32[32,1024]{1,0:T(8,128)} %reduce-scatter.3.cloned.1.call-done) | copy-start | bytes 393220
  254.5 12.2 %copy-start.21 = (s32[32]{0:T(128)S(1)}, s32[32]{0:T(128)}, u32[]{:S(2)}) copy-start(s32[32]{0:T(128)} %copy-done.20) | copy-start | bytes 388
  266.5 282.2 %reduce-scatter.5.cloned.1.call-start = ((), (), s32[]{:S(2)}) async-start(), calls=%async_computation.6 | async-start | bytes 18874368 | tf_op jit(solution)/shard_map/reduce_scatter | solution.py:191
  322.3 15.7 %copy-start.4 = (bf16[512,8192]{1,0:T(8,128)(2,1)}, bf16[512,8192]{1,0:T(8,128)(2,1)S(1)}, u32[]{:S(2)}) copy-start(bf16[512,8192]{1,0:T(8,128)(2,1)S(1)} %multiply_convert_fusion) | copy-start | bytes 25165828
  322.3 5.2 copy-start.5
  338.0 7.1 %copy-start.6 = (f32[8192,128]{0,1:T(8,128)S(1)}, f32[8192,128]{0,1:T(8,128)}, u32[]{:S(2)}) copy-start(f32[8192,128]{0,1:T(8,128)} %fusion.88) | copy-start | bytes 12582916
  338.0 7.1 %copy-start.7 = (f32[8192,128]{0,1:T(8,128)S(1)}, f32[8192,128]{0,1:T(8,128)}, u32[]{:S(2)}) copy-start(f32[8192,128]{0,1:T(8,128)} %fusion.85) | copy-start | bytes 12582916
  338.0 8.6 %copy-start.8 = (f32[8192,128]{0,1:T(8,128)S(1)}, f32[8192,128]{0,1:T(8,128)}, u32[]{:S(2)}) copy-start(f32[8192,128]{0,1:T(8,128)} %fusion.54) | copy-start | bytes 12582916
  356.0 7.1 %copy-start.11 = (bf16[8192,256]{0,1:T(8,128)(2,1)S(1)}, bf16[8192,256]{0,1:T(8,128)(2,1)}, u32[]{:S(2)}) copy-start(bf16[8192,256]{0,1:T(8,128)(2,1)} %all-gather.4.cloned.1.call-done) | copy-start | bytes 12582916
  363.1 7.2 %copy-start.15 = (f32[512,64]{0,1:T(8,128)S(1)}, f32[512,64]{0,1:T(8,128)}, u32[]{:S(2)}) copy-start(f32[512,64]{0,1:T(8,128)} %get-tuple-element.38) | copy-start | bytes 393220
  363.1 188.6 %copy-start.13 = (f32[1024,64]{0,1:T(8,128)S(1)}, f32[1024,64]{0,1:T(8,128)}, u32[]{:S(2)}) copy-start(f32[1024,64]{0,1:T(8,128)} %copy-done.12) | copy-start | bytes 786436
  363.1 188.5 %copy-start.14 = (f32[1024,64]{0,1:T(8,128)S(1)}, f32[1024,64]{0,1:T(8,128)}, u32[]{:S(2)}) copy-start(f32[1024,64]{0,1:T(8,128)} %get-tuple-element.35) | copy-start | bytes 786436
  370.2 183.1 %copy-start.1 = (bf16[256,1024]{1,0:T(8,128)(2,1)S(1)}, bf16[256,1024]{1,0:T(8,128)(2,1)}, u32[]{:S(2)}) copy-start(bf16[256,1024]{1,0:T(8,128)(2,1)} %param.18) | copy-start | bytes 1572868
Sparse Core Ops, SparseCore 0:
  12.0 74.0 all-gather.3
  88.4 69.2 all-gather.5
  172.2 61.7 reduce-scatter.2
  266.6 31.0 all-gather.7
  354.9 193.6 reduce-scatter.4
where the time goes:
time: 570 us; the launch traced here: 561 us
  waiting for transfers between devices  356 us (62%)
  matrix products  109 us (19%)
  other arithmetic  58.8 us (10%)
  between operations  19.5 us (3%)
  local copies, waits for them, and re-layouts  17.6 us (3%)
    reduce_scatter x1, waiting for transfers between devices, shards(): lax.psum_scatter(jnp.concatenate(key_parts + value_parts, axis=1), 'ctx',...  177 us
    all_gather x1, waiting for transfers between devices, shards(): lax.all_gather(rotated_key, 'ctx', axis=0, tiled=True)  67 us
    reduce_scatter x1, waiting for transfers between devices, shards(): lax.psum_scatter(jnp.dot(grouped_out, in_proj, preferred_element_type=jnp...  60.6 us
    all_gather x1, waiting for transfers between devices, shards(): lax.all_gather(low_grad, 'frame', axis=0, tiled=True)  30.9 us
    dot_general x4, matrix products, contract_rows(): lax.dot_general(left, right, (((0,), (0,)), ((), ())), preferred_element_...  23.6 us
    all_gather x1, waiting for transfers between devices, shards(): lax.all_gather(values, 'ctx', axis=0, tiled=True)  19.5 us
    dot_general x2, matrix products, shards(): jnp.dot(out_grad[:, lower:lower + HD], whole_value[:, lower:lower + HD].T...  19.1 us
    reduce_sum x2, other arithmetic, shards(): total = jnp.sum(jnp.exp(scores - largest[:, None]), axis=1)  16.8 us
  transfers between devices with their start and end apart: 5, of which 5 were waited for; matrix products, arithmetic and copies ran while one was open for 13% of the time, Pallas kernels for 0%

commit v1 on v0

--- a/solution.py
+++ b/solution.py
@@ -91,7 +91,9 @@
     rotated_query = rotate(queries.astype(jnp.float32), query_position, False).astype(jnp.bfloat16)
     rotated_key = rotate(keys.astype(jnp.float32), key_position, False).astype(jnp.bfloat16)
     whole_key, whole_value = (
-        lax.all_gather(rotated_key, "ctx", axis=0, tiled=True),
+        jnp.concatenate(
+            lax.all_to_all(jnp.stack([rotated_key] * lax.axis_size("ctx")), "ctx", 0, 0), axis=0
+        ),
         lax.all_gather(values, "ctx", axis=0, tiled=True),
     )
     out_list, log_list, weight_list = ([], [], [])

time: 570 us -> 546 us (0.958)
  waiting for transfers between devices: 356 us -> 333 us
  starting transfers between devices: 0.37 us -> 8.35 us
  other arithmetic: 58.8 us -> 52.5 us
    all_gather x1 -> x0, waiting for transfers between devices: 67 us -> none  [shards(): lax.all_gather(rotated_key, 'ctx', axis=0, tiled=True)]
    all_to_all x0 -> x1, waiting for transfers between devices: none -> 63.6 us  [shards(): lax.all_to_all(jnp.stack([rotated_key] * lax.axis_size('ctx')), 'ctx', 0, 0)]
    all_gather x1, waiting for transfers between devices: 19.5 us -> 0.02 us  [shards(): lax.all_gather(values, 'ctx', axis=0, tiled=True)]
    all_to_all x0 -> x1, starting transfers between devices: none -> 7.72 us  [shards(): lax.all_to_all(jnp.stack([rotated_key] * lax.axis_size('ctx')), 'ctx', 0, 0)]
  transfers between devices with their start and end apart: 5 -> 5, of which waited for: 5 -> 4; matrix products, arithmetic and copies ran while one was open for 13% -> 12% of each run, Pallas kernels for 0% -> 0%
where the time goes in v1:
time: 546 us; the launch traced here: 543 us
  waiting for transfers between devices  333 us (61%)
  matrix products  111 us (20%)
  other arithmetic  52.5 us (10%)
  between operations  19.6 us (4%)
  local copies, waits for them, and re-layouts  18.4 us (3%)
  starting transfers between devices  8.35 us (2%)
    reduce_scatter x1, waiting for transfers between devices, shards(): lax.psum_scatter(jnp.concatenate(key_parts + value_parts, axis=1), 'ctx',...  177 us
    all_to_all x1, waiting for transfers between devices, shards(): lax.all_to_all(jnp.stack([rotated_key] * lax.axis_size('ctx')), 'ctx', 0, 0)  63.6 us
    reduce_scatter x1, waiting for transfers between devices, shards(): lax.psum_scatter(jnp.dot(grouped_out, in_proj, preferred_element_type=jnp...  60.6 us
    all_gather x1, waiting for transfers between devices, shards(): lax.all_gather(low_grad, 'frame', axis=0, tiled=True)  30.7 us
    dot_general x4, matrix products, contract_rows(): lax.dot_general(left, right, (((0,), (0,)), ((), ())), preferred_element_...  23.5 us
    dot_general x2, matrix products, shards(): jnp.dot(out_grad[:, lower:lower + HD], whole_value[:, lower:lower + HD].T...  19.1 us
    dot_general x2, matrix products, head_scores(): jnp.dot(query_head, key_head.T, preferred_element_type=jnp.float32)  17.7 us
    reduce_sum x2, other arithmetic, shards(): total = jnp.sum(jnp.exp(scores - largest[:, None]), axis=1)  16.3 us
  transfers between devices with their start and end apart: 5, of which 4 were waited for; matrix products, arithmetic and copies ran while one was open for 12% of the time, Pallas kernels for 0%

profile of v1, /device:TPU:0, one launch (start us, length us, event | category | flops | bytes accessed | tf_op | source)
XLA Modules:
  0.0 542.8 jit_solution(8278287991324596138)
XLA Ops:
  10.0 2.2 stack.2
  12.2 7.7 %all-to-all-start = ((bf16[8,1024,256]{2,1,0:T(8,128)(2,1)}), bf16[8,1024,256]{2,1,0:T(8,128)(2,1)}, u32[]{:S(2)}, u32[]{:S(2)}) async-start(bf16[8,1024,256]{2,1,0:T(8,128)(2,1)} %stack.2), calls=%async_computation | async-start | bytes 8388608 | tf_op jit(solution)/shard_map/all_to_all | solution.py:95
  22.6 63.6 %all-to-all-done = bf16[8,1024,256]{2,1,0:T(8,128)(2,1)} async-done(((bf16[8,1024,256]{2,1,0:T(8,128)(2,1)}), bf16[8,1024,256]{2,1,0:T(8,128)(2,1)}, u32[]{:S(2)}, u32[]{:S(2)}) %all-to-all-start) | async-done | bytes 4194336 | tf_op jit(solution)/shard_map/all_to_all | solution.py:95
  86.2 9.0 %fusion.94 = (f32[512]{0:T(512)S(1)}, f32[512,8192]{1,0:T(8,128)}) fusion(bf16[8192,256]{1,0:T(8,128)(2,1)} %bitcast.2, bf16[512,256]{0,1:T(8,128)(2,1)S(1)} %bitcast.42, pred[8192]{0:T(1024)(128)(4,1)S(1)} %lt.69), kind=kOutput, calls=%fused_computation.162 | convolution fusion | flops 1086324224 | bytes 19015680 | tf_op jit(solution)/shard_map/dot_general | solution.py:40
  95.2 8.1 %exponential_reduce_fusion = f32[512]{0:T(512)S(1)} fusion(f32[512,8192]{1,0:T(8,128)} %get-tuple-element.42, f32[512]{0:T(512)S(1)} %get-tuple-element.41), kind=kLoop, calls=%fused_computation.6 | loop fusion | flops 8388096 | bytes 16781312 | tf_op jit(solution)/shard_map/reduce_sum | solution.py:106
  103.3 8.8 %fusion.95 = (f32[512]{0:T(512)S(1)}, f32[512,8192]{1,0:T(8,128)}) fusion(bf16[8192,256]{1,0:T(8,128)(2,1)} %bitcast.2, bf16[512,256]{0,1:T(8,128)(2,1)S(1)} %bitcast.43, pred[8192]{0:T(1024)(128)(4,1)S(1)} %lt.69), kind=kOutput, calls=%fused_computation.163 | convolution fusion | flops 1086324224 | bytes 19015680 | tf_op jit(solution)/shard_map/dot_general | solution.py:40
  112.1 8.2 %exponential_reduce_fusion.1 = f32[512]{0:T(512)S(1)} fusion(f32[512,8192]{1,0:T(8,128)} %get-tuple-element.44, f32[512]{0:T(512)S(1)} %get-tuple-element.43), kind=kLoop, calls=%fused_computation.9 | loop fusion | flops 8388096 | bytes 16781312 | tf_op jit(solution)/shard_map/reduce_sum | solution.py:106
  120.2 9.8 %fusion.1 = bf16[512,8192]{1,0:T(8,128)(2,1)} fusion(f32[512,8192]{1,0:T(8,128)} %get-tuple-element.42, f32[512]{0:T(512)S(1)} %log_add_fusion), kind=kLoop, calls=%fused_computation.12 | loop fusion | flops 8388608 | bytes 25167872 | tf_op jit(solution)/shard_map/convert_element_type | solution.py:111
  130.1 3.8 copy-done.2
  133.9 5.1 fusion
  139.0 7.0 %fusion.18 = bf16[512,128]{0,1:T(8,128)(2,1)S(1)} fusion(bf16[512,8192]{1,0:T(8,128)(2,1)} %fusion.1, bf16[8192,256]{1,0:T(8,128)(2,1)} %all-gather.3.cloned.1.call-done), kind=kOutput, calls=%fused_computation.29 | convolution fusion | flops 1073807360 | bytes 10616832 | tf_op jit(solution)/shard_map/dot_general | solution.py:110
  146.0 4.5 fusion.15
  151.4 1.8 fusion.98
  154.6 60.6 %reduce-scatter.3.cloned.1.call-done = f32[32,1024]{1,0:T(8,128)} async-done(((f32[512,1024]{1,0:T(8,128)}), f32[32,1024]{1,0:T(8,128)}) %reduce-scatter.3.cloned.1.call-update) | async-done | bytes 131088 | tf_op jit(solution)/shard_map/reduce_scatter | solution.py:137
  217.3 5.0 fusion.61
  222.4 4.9 fusion.22
  235.8 11.0 %multiply_reduce_fusion.2 = (f32[32]{0:T(128)S(1)}, f32[32,1024]{1,0:T(8,128)S(1)}) fusion(f32[32,1024]{1,0:T(8,128)S(1)} %copy-done.9, f32[32]{0:T(128)S(1)} %broadcast_multiply_fusion, bf16[1024,4096]{1,0:T(8,128)(2,1)} %param.19, f32[32,4096]{1,0:T(8,128)S(1)} %fusion.61, bf16[4096,1024]{1,0:T(8,128)(2,1)} %param.20, f32[1024]{0:T(1024)S(1)} %add_divide_fusion, ...), kind=kOutput, calls=%fused_computation.89 | convolution fusion | flops 539820032 | bytes 17568128 | tf_op jit(solution)/shard_map/transpose(jvp())/dot_general | solution.py:54
  248.0 30.7 %all-gather.5.cloned.1.call-done = bf16[512,1024]{1,0:T(8,128)(2,1)} async-done(((bf16[32,1024]{1,0:T(8,128)(2,1)}), bf16[512,1024]{1,0:T(8,128)(2,1)}) %all-gather.5.cloned.1.call-update) | async-done | bytes 1048592 | tf_op jit(solution)/shard_map/all_gather | solution.py:150
  278.8 1.7 convolution_convert_fusion.1
  281.2 6.6 %fusion.88 = f32[8192,128]{0,1:T(8,128)} fusion(bf16[512,8192]{1,0:T(8,128)(2,1)} %fusion, bf16[512,256]{1,0:T(8,128)(2,1)S(1)} %bitcast.34), kind=kOutput, calls=%fused_computation.156 | convolution fusion | flops 1073741824 | bytes 12713984 | tf_op jit(solution)/shard_map/dot_general | solution.py:47
  287.8 6.6 %fusion.85 = f32[8192,128]{0,1:T(8,128)} fusion(bf16[512,8192]{1,0:T(8,128)(2,1)} %fusion.1, bf16[512,256]{1,0:T(8,128)(2,1)S(1)} %bitcast.35), kind=kOutput, calls=%fused_computation.153 | convolution fusion | flops 1073741824 | bytes 12713984 | tf_op jit(solution)/shard_map/dot_general | solution.py:47
  294.8 8.7 %multiply_convert_fusion = bf16[512,8192]{1,0:T(8,128)(2,1)S(1)} fusion(f32[512,8192]{1,0:T(8,128)} %get-tuple-element.42, f32[512]{0:T(512)S(1)} %multiply_reduce_fusion, f32[512]{0:T(512)S(1)} %log_add_fusion, bf16[8192,256]{1,0:T(8,128)(2,1)} %all-gather.3.cloned.1.call-done, bf16[512,256]{1,0:T(8,128)(2,1)S(1)} %bitcast.37), kind=kOutput, calls=%fused_computation.3 | convolution fusion | flops 1094713344 | bytes 27398144 | tf_op jit(solution)/shard_map/dot_general | solution.py:169
  303.5 3.4 fusion.54
  306.8 1.8 copy-done.5
  308.7 10.4 %multiply_convert_fusion.1 = bf16[512,8192]{1,0:T(8,128)(2,1)} fusion(f32[512,8192]{1,0:T(8,128)} %get-tuple-element.44, f32[512]{0:T(512)S(1)} %multiply_reduce_fusion.1, f32[512]{0:T(512)S(1)} %log_add_fusion.1, bf16[8192,256]{1,0:T(8,128)(2,1)S(1)} %copy-done.5, bf16[512,256]{1,0:T(8,128)(2,1)S(1)} %bitcast.38), kind=kOutput, calls=%fused_computation.4 | convolution fusion | flops 1094713344 | bytes 27398144 | tf_op jit(solution)/shard_map/dot_general | solution.py:169
  319.1 6.9 %fusion.57 = f32[8192,128]{0,1:T(8,128)} fusion(bf16[512,8192]{1,0:T(8,128)(2,1)} %multiply_convert_fusion.1, bf16[512,256]{0,1:T(8,128)(2,1)S(1)} %bitcast.45), kind=kOutput, calls=%fused_computation.96 | convolution fusion | flops 1073741824 | bytes 12713984 | tf_op jit(solution)/shard_map/dot_general | solution.py:47
  326.1 1.6 copy-done.8
  327.7 8.2 %pad_maximum_fusion = f32[8192,512]{0,1:T(8,128)} fusion(f32[8192,128]{0,1:T(8,128)S(1)} %copy-done.7, f32[8192,128]{0,1:T(8,128)S(1)} %copy-done.6, f32[8192,128]{0,1:T(8,128)S(1)} %copy-done.8, f32[8192,128]{0,1:T(8,128)} %fusion.57), kind=kLoop, calls=%fused_computation.2 | loop fusion | flops 12582912 | bytes 33554432 | tf_op jit(solution)/shard_map/concatenate | solution.py:194
  337.2 6.9 %fusion.6 = f32[512,128]{0,1:T(8,128)S(1)} fusion(bf16[512,8192]{1,0:T(8,128)(2,1)} %copy-done.3, bf16[8192,256]{1,0:T(8,128)(2,1)} %bitcast.2), kind=kOutput, calls=%fused_computation.18 | convolution fusion | flops 1073741824 | bytes 10747904 | tf_op jit(solution)/shard_map/dot_general | solution.py:178
  344.1 7.6 %fusion.12 = f32[512,128]{0,1:T(8,128)S(1)} fusion(bf16[512,8192]{1,0:T(8,128)(2,1)} %multiply_convert_fusion.1, bf16[8192,256]{1,0:T(8,128)(2,1)} %bitcast.2), kind=kOutput, calls=%fused_computation.24 | convolution fusion | flops 1073741824 | bytes 10747904 | tf_op jit(solution)/shard_map/dot_general | solution.py:178
  352.9 177.4 %reduce-scatter.5.cloned.1.call-done = f32[1024,512]{0,1:T(8,128)} async-done(((f32[8192,512]{0,1:T(8,128)}), f32[1024,512]{0,1:T(8,128)}) %reduce-scatter.5.cloned.1.call-update) | async-done | bytes 2097168 | tf_op jit(solution)/shard_map/reduce_scatter | solution.py:193
  530.2 1.7 fusion.92
  (100 shorter events, 21.8 us)
Async XLA Ops:
  7.2 144.2 %copy-start = (bf16[256,1024]{1,0:T(8,128)(2,1)S(1)}, bf16[256,1024]{1,0:T(8,128)(2,1)}, u32[]{:S(2)}) copy-start(bf16[256,1024]{1,0:T(8,128)(2,1)} %param.18) | copy-start | bytes 1572868
  9.7 11.3 %copy-start.14 = (s32[32]{0:T(128)S(1)}, s32[32]{0:T(128)}, u32[]{:S(2)}) copy-start(s32[32]{0:T(128)} %param.15) | copy-start | bytes 388
  9.7 11.5 %copy-start.12 = (s32[512]{0:T(512)S(1)}, s32[512]{0:T(512)}, u32[]{:S(2)}) copy-start(s32[512]{0:T(512)} %param.16) | copy-start | bytes 6148
  9.7 11.8 %copy-start.10 = (bf16[512,256]{1,0:T(8,128)(2,1)S(1)}, bf16[512,256]{1,0:T(8,128)(2,1)}, u32[]{:S(2)}) copy-start(bf16[512,256]{1,0:T(8,128)(2,1)} %param.12) | copy-start | bytes 786436
  9.7 11.9 %copy-start.13 = (s32[32]{0:T(128)S(1)}, s32[32]{0:T(128)}, u32[]{:S(2)}) copy-start(s32[32]{0:T(128)} %param.17) | copy-start | bytes 388
  12.2 74.0 %all-to-all-start = ((bf16[8,1024,256]{2,1,0:T(8,128)(2,1)}), bf16[8,1024,256]{2,1,0:T(8,128)(2,1)}, u32[]{:S(2)}, u32[]{:S(2)}) async-start(bf16[8,1024,256]{2,1,0:T(8,128)(2,1)} %stack.2), calls=%async_computation | async-start | bytes 8388608 | tf_op jit(solution)/shard_map/all_to_all | solution.py:95
  19.9 119.1 %all-gather.3.cloned.1.call-start = ((), (), s32[]{:S(2)}) async-start(), calls=%async_computation.3 | async-start | bytes 4718592 | tf_op jit(solution)/shard_map/all_gather | solution.py:97
  20.6 194.5 %reduce-scatter.3.cloned.1.call-start = ((), (), s32[]{:S(2)}) async-start(), calls=%async_computation.4 | async-start | bytes 2228224 | tf_op jit(solution)/shard_map/reduce_scatter | solution.py:137
  120.2 13.7 %copy-start.2 = (f32[512,8192]{1,0:T(8,128)S(1)}, f32[512,8192]{1,0:T(8,128)}, u32[]{:S(2)}) copy-start(f32[512,8192]{1,0:T(8,128)} %get-tuple-element.44) | copy-start | bytes 50331652
  139.0 7.0 %copy-start.4 = (bf16[512,8192]{1,0:T(8,128)(2,1)S(1)}, bf16[512,8192]{1,0:T(8,128)(2,1)}, u32[]{:S(2)}) copy-start(bf16[512,8192]{1,0:T(8,128)(2,1)} %fusion) | copy-start | bytes 25165828
  153.2 125.6 %all-gather.5.cloned.1.call-start = ((), (), s32[]{:S(2)}) async-start(), calls=%async_computation.5 | async-start | bytes 1114112 | tf_op jit(solution)/shard_map/all_gather | solution.py:150
  222.3 8.9 %copy-start.11 = (f32[1024]{0:T(1024)S(1)}, f32[1024]{0:T(1024)}, u32[]{:S(2)}) copy-start(f32[1024]{0:T(1024)} %param.21) | copy-start | bytes 12292
  222.3 13.4 %copy-start.9 = (f32[32,1024]{1,0:T(8,128)S(1)}, f32[32,1024]{1,0:T(8,128)}, u32[]{:S(2)}) copy-start(f32[32,1024]{1,0:T(8,128)} %reduce-scatter.3.cloned.1.call-done) | copy-start | bytes 393220
  247.8 282.4 %reduce-scatter.5.cloned.1.call-start = ((), (), s32[]{:S(2)}) async-start(), calls=%async_computation.6 | async-start | bytes 18874368 | tf_op jit(solution)/shard_map/reduce_scatter | solution.py:193
  303.4 15.7 %copy-start.3 = (bf16[512,8192]{1,0:T(8,128)(2,1)}, bf16[512,8192]{1,0:T(8,128)(2,1)S(1)}, u32[]{:S(2)}) copy-start(bf16[512,8192]{1,0:T(8,128)(2,1)S(1)} %multiply_convert_fusion) | copy-start | bytes 25165828
  303.5 5.2 copy-start.5
  319.1 7.0 %copy-start.6 = (f32[8192,128]{0,1:T(8,128)S(1)}, f32[8192,128]{0,1:T(8,128)}, u32[]{:S(2)}) copy-start(f32[8192,128]{0,1:T(8,128)} %fusion.88) | copy-start | bytes 12582916
  319.1 7.0 %copy-start.7 = (f32[8192,128]{0,1:T(8,128)S(1)}, f32[8192,128]{0,1:T(8,128)}, u32[]{:S(2)}) copy-start(f32[8192,128]{0,1:T(8,128)} %fusion.85) | copy-start | bytes 12582916
  319.1 8.6 %copy-start.8 = (f32[8192,128]{0,1:T(8,128)S(1)}, f32[8192,128]{0,1:T(8,128)}, u32[]{:S(2)}) copy-start(f32[8192,128]{0,1:T(8,128)} %fusion.54) | copy-start | bytes 12582916
  351.7 183.2 %copy-start.1 = (bf16[256,1024]{1,0:T(8,128)(2,1)S(1)}, bf16[256,1024]{1,0:T(8,128)(2,1)}, u32[]{:S(2)}) copy-start(bf16[256,1024]{1,0:T(8,128)(2,1)} %param.18) | copy-start | bytes 1572868
Sparse Core Ops, SparseCore 0:
  23.1 106.2 all-gather.2
  153.3 61.7 reduce-scatter.2
  247.9 30.8 all-gather.4
  336.0 194.1 reduce-scatter.4
